TPU v7x, 256 devices: a whole 4x4x8 slice. The times are simulated.
256 devices in a mesh: dp: 32 (over z, x), mp: 8 (over y, core).
Axes of the slice: x: 4, y: 4, z: 8, core: 2. Of those that a mesh axis runs over, the one named last changes fastest.
Arguments:
- tokens: bfloat16 [32768, 8192], P('dp', 'mp'), may hold values from -6 to 6
- value_weight: bfloat16 [8192, 1024], P('mp'), may hold values from -0.0625 to 0.0625
- adapter_down_panels: bfloat16 [96, 64, 8192], P('dp', None, 'mp'), may hold values from -0.0625 to 0.0625
- adapter_up_panels: bfloat16 [96, 64, 1024], P('dp', None, 'mp'), may hold values from -0.75 to 0.75
- cotangent: bfloat16 [32768, 1024], P('dp', 'mp'), may hold values from -6 to 6
- block_list_entry: int32 [1024], P('dp'), may hold values from 0 to 31, as said below
- device_tenant_list: int32 [1024], P('dp'), may hold values from 0 to 95, as said below
- tenant_location_map: int32 [96], replicated, may hold values from 0 to 95, as said below
Outputs:
- values: bfloat16 [32768, 1024], P('dp', 'mp')
- token_gradient: bfloat16 [32768, 8192], P('dp', 'mp')
- grad_a: bfloat16 [96, 64, 8192], P('dp', None, 'mp')
- grad_b: bfloat16 [96, 64, 1024], P('dp', None, 'mp')
Inputs may be any that keep to these rules, and one draw needn't show every extreme that they name: `device_tenant_list`: each entry names a tenant; no tenant stands twice in one list. Of one device's 32 entries, at most 2 name tenants whose storage location tenant_location_map[t] lies on one dp index (tenant_location_map[t] // 3), and every device's list has 2 entries on some one dp index. A permutation: tenant t's panels are row tenant_location_map[t] of adapter_down_panels and adapter_up_panels. `block_list_entry`: every entry of a device's tenant list is named by at least one of that device's row blocks.
All inputs are finite; a program needn't handle non-finite values.
Results may differ from a plain program's by a relative error of at most 0.0057.
Values may be sent and summed in bfloat16 or wider, within the bound.
A program may use at most 128 MiB of HBM per device.

v0:
```python
import jax
import jax.numpy as jnp
import numpy as np
from jax import lax
from jax.sharding import Mesh
from jax.sharding import PartitionSpec as P

MOST = 2
DP = ("dz", "dx")


def earlier_same(group):
    count = group.shape[-1]
    ids = jnp.arange(count, dtype=jnp.int32)
    same = (group[..., :, None] == group[..., None, :]) & (ids[:, None] > ids[None, :])
    return jnp.sum(same.astype(jnp.int32), axis=-1)


def shards(
    tokens,
    value_weight,
    adapter_down_panels,
    adapter_up_panels,
    cotangent,
    block_list_entry,
    device_tenant_list,
    tenant_location_map,
):
    rows, width_loc = tokens.shape
    stored, rank, _ = adapter_down_panels.shape
    out_loc = adapter_up_panels.shape[2]
    blocks = block_list_entry.shape[0]
    blk = rows // blocks
    n_z = lax.axis_size("dz")
    n_x = lax.axis_size("dx")
    per_x = min(MOST * n_z, blocks)
    capacity = n_x * per_x
    my_x = lax.axis_index("dx")
    column = n_z * stored
    tenant = jnp.take(device_tenant_list, block_list_entry, mode="clip")
    location = jnp.take(tenant_location_map, tenant, mode="clip")
    owner_x = location // stored % n_x
    position = jnp.clip(owner_x * per_x + earlier_same(owner_x), 0, capacity - 1)
    slot_ids = jnp.arange(capacity, dtype=jnp.int32)
    block_ids = jnp.arange(blocks, dtype=jnp.int32)
    source = jnp.sum(
        jnp.where(position[None, :] == slot_ids[:, None], block_ids[None, :], 0), axis=1
    )
    base_part = lax.dot_general(
        value_weight, tokens, (((0,), (1,)), ((), ())), preferred_element_type=jnp.float32
    )
    location_tied, base_part = lax.optimization_barrier((location, base_part))
    base_t = lax.psum_scatter(base_part, "mp", scatter_dimension=0, tiled=True)
    x_location = lax.all_gather(location_tied, "dx", axis=0, tiled=False)
    x_owner_x = x_location // stored % n_x
    x_rank = earlier_same(x_owner_x)
    in_column = x_location // stored // n_x * stored + x_location % stored
    mine = x_owner_x == my_x
    slot_panel = (
        jnp.stack(
            [
                jnp.sum(jnp.where(mine & (x_rank == c), in_column + 1, 0), axis=1)
                for c in range(per_x)
            ],
            axis=1,
        ).reshape(capacity)
        - 1
    )
    panel_ids = jnp.arange(column, dtype=jnp.int32)
    slot_of = x_rank + (jnp.arange(n_x, dtype=jnp.int32) * per_x)[:, None]
    panel_slot = (
        jnp.sum(
            jnp.where(
                mine[None, :, :] & (in_column[None, :, :] == panel_ids[:, None, None]),
                slot_of[None, :, :] + 1,
                0,
            ),
            axis=2,
        )
        - 1
    )
    panel_used = panel_slot >= 0
    panel_slot = jnp.clip(panel_slot, 0, capacity - 1)
    both_col = lax.all_gather(
        jnp.concatenate([adapter_down_panels, adapter_up_panels], axis=2), "dz", axis=0, tiled=True
    )
    down_col = both_col[:, :, :width_loc]
    up_col = both_col[:, :, width_loc:]
    n_mp = lax.axis_size("mp")
    token_blocks = tokens.reshape(blocks, blk, width_loc)
    cot_blocks = cotangent.reshape(blocks, blk, out_loc)
    send = jnp.concatenate(
        [
            jnp.take(token_blocks, source, axis=0, mode="clip"),
            jnp.take(cot_blocks, source, axis=0, mode="clip"),
        ],
        axis=2,
    )
    recv = lax.all_to_all(send, "dx", split_axis=0, concat_axis=0, tiled=True)
    tok_recv = recv[:, :, :width_loc]
    cot_recv = recv[:, :, width_loc:]
    panel_at = jnp.clip(slot_panel, 0, column - 1)
    down_sel = jnp.take(down_col, panel_at, axis=0, mode="clip")
    up_sel = jnp.take(up_col, panel_at, axis=0, mode="clip")
    down_part = jnp.einsum("snd,srd->snr", tok_recv, down_sel, preferred_element_type=jnp.float32)
    up_part = jnp.einsum("snc,src->snr", cot_recv, up_sel, preferred_element_type=jnp.float32)
    both = lax.psum(jnp.stack([down_part, up_part]), "mp").astype(jnp.bfloat16)
    cot_parts = lax.all_gather(cotangent, "mp", axis=0, tiled=False)
    down_low = both[0]
    up_grad = both[1]
    adapter_out = jnp.einsum("snr,src->snc", down_low, up_sel, preferred_element_type=jnp.float32)
    adapter_bwd = jnp.einsum("snr,srd->snd", up_grad, down_sel, preferred_element_type=jnp.float32)
    back_send = jnp.concatenate(
        [adapter_bwd.astype(jnp.bfloat16), adapter_out.astype(jnp.bfloat16)], axis=2
    )
    back = lax.all_to_all(back_send, "dx", split_axis=0, concat_axis=0, tiled=True)

    def by_panel(small):
        small_p = jnp.take(small, panel_slot.reshape(-1), axis=0, mode="clip").reshape(
            column, n_x, blk, rank
        )
        small_p = jnp.where(panel_used[:, :, None, None], small_p, jnp.zeros_like(small_p))
        return small_p.reshape(column, n_x * blk, rank)

    rows_p = jnp.take(recv, panel_slot.reshape(-1), axis=0, mode="clip").reshape(
        column, n_x * blk, width_loc + out_loc
    )
    grad_up = jnp.einsum(
        "pnr,pnd->prd", by_panel(up_grad), rows_p, preferred_element_type=jnp.float32
    )
    grad_low = jnp.einsum(
        "pnr,pnd->prd", by_panel(down_low), rows_p, preferred_element_type=jnp.float32
    )
    feature = jnp.arange(width_loc + out_loc, dtype=jnp.int32)[None, None, :]
    grads_col = jnp.where(feature < width_loc, grad_up, grad_low)
    grads = lax.psum_scatter(
        grads_col.astype(jnp.bfloat16).reshape(column * rank, width_loc + out_loc),
        "dz",
        scatter_dimension=0,
        tiled=True,
    )
    grad_a = grads[:, :width_loc]
    grad_b = grads[:, width_loc:]
    grad_a = grad_a.astype(jnp.bfloat16).reshape(stored, rank, width_loc)
    grad_b = grad_b.astype(jnp.bfloat16).reshape(stored, rank, out_loc)
    base_bwd = jnp.einsum(
        "krc,dkc->rd",
        cot_parts,
        value_weight.reshape(width_loc, n_mp, out_loc),
        preferred_element_type=jnp.float32,
    )
    base_bwd = lax.optimization_barrier(base_bwd)
    mine_back = jnp.take(back, position, axis=0, mode="clip").reshape(rows, width_loc + out_loc)
    values = (base_t.T + mine_back[:, width_loc:].astype(jnp.float32)).astype(jnp.bfloat16)
    token_gradient = (base_bwd + mine_back[:, :width_loc].astype(jnp.float32)).astype(jnp.bfloat16)
    return (values, token_gradient, grad_a, grad_b)


def split_dp(mesh):
    devices = np.asarray(mesh.devices)
    n_dp, n_mp = devices.shape
    try:
        n_x = len({tuple(d.coords)[0] for d in devices[:, 0]})
    except (AttributeError, TypeError):
        n_x = 1
    if n_x < 1 or n_dp % n_x:
        n_x = 1
    return Mesh(devices.reshape(n_dp // n_x, n_x, n_mp), ("dz", "dx", "mp"))


def solution(mesh):
    in_specs = (
        P(DP, "mp"),
        P("mp", None),
        P(DP, None, "mp"),
        P(DP, None, "mp"),
        P(DP, "mp"),
        P(DP),
        P(DP),
        P(),
    )
    out_specs = (P(DP, "mp"), P(DP, "mp"), P(DP, None, "mp"), P(DP, None, "mp"))
    return jax.shard_map(
        shards, mesh=split_dp(mesh), in_specs=in_specs, out_specs=out_specs, check_vma=False
    )
```

profile of v0, /device:TPU:224, one launch (start us, length us, event | category | flops | bytes accessed | tf_op | source)
XLA Modules:
  0.0 285.4 jit_solution(7799087887903923186)
XLA Ops:
  7.2 2.0 pad_maximum_fusion.3
  10.7 1.4 gather_fusion
  12.0 1.4 gather_fusion.1
  13.4 6.0 %fusion.27 = f32[1024,1024]{1,0:T(8,128)} fusion(bf16[1024,1024]{1,0:T(8,128)(2,1)} %param.9, bf16[1024,1024]{1,0:T(8,128)(2,1)S(1)} %copy-done), kind=kOutput, calls=%fused_computation.109 | convolution fusion | flops 2147483648 | bytes 8388608 | tf_op jit(solution)/shard_map/dot_general | solution.py:49
  21.0 2.8 gather_fusion.2
  23.8 4.9 %pad_maximum_fusion = bf16[64,32,1152]{2,1,0:T(8,128)(2,1)} fusion(bf16[64,32,128]{2,1,0:T(8,128)(2,1)S(1)} %gather_fusion.3, bf16[64,32,1024]{2,1,0:T(8,128)(2,1)} %gather_fusion.2), kind=kLoop, calls=%fused_computation.11 | loop fusion | flops 9437184 | bytes 9437184 | tf_op jit(solution)/shard_map/concatenate | solution.py:92
  28.8 5.1 %all-to-all-start = ((bf16[64,32,1152]{2,1,0:T(8,128)(2,1)}), bf16[64,32,1152]{2,1,0:T(8,128)(2,1)}, u32[]{:S(2)}, u32[]{:S(2)}) async-start(bf16[64,32,1152]{2,1,0:T(8,128)(2,1)} %pad_maximum_fusion), calls=%async_computation.1 | async-start | bytes 9437184 | tf_op jit(solution)/shard_map/all_to_all | solution.py:99
  35.4 55.9 %all-reduce = s32[128]{0:T(128)S(1)} all-reduce(s32[128]{0:T(128)S(1)} %dynamic-update-slice), channel_id=2, replica_groups=mesh['dz'=8,'dx'=4,'mp'=8] {'dx'}, use_global_device_ids=true, to_apply=%add | all-reduce | flops 128 | bytes 1024
  94.7 8.8 %gather_fusion.8 = bf16[96,32,1152]{2,1,0:T(8,128)(2,1)} fusion(bf16[64,32,1152]{2,1,0:T(8,128)(2,1)} %all-to-all-done, s32[1024]{0:T(1024)S(1)} %pad_clamp_fusion), kind=kCustom, calls=%fused_computation.8 | custom fusion | bytes 14156160 | tf_op jit(solution)/shard_map/jit(_take)/gather | solution.py:125
  103.5 1.0 slice.63
  105.3 4.1 %slice.61 = bf16[24,64,1024]{2,1,0:T(8,128)(2,1)} slice(bf16[24,64,1152]{2,1,0:T(8,128)(2,1)} %all-gather.5.cloned.1.call-done), slice={[0:24], [0:64], [0:1024]} | slice | bytes 6291456 | tf_op jit(solution)/shard_map/slice | solution.py:87
  109.4 7.5 %gather_fusion.4 = bf16[64,64,1024]{2,1,0:T(8,128)(2,1)} fusion(bf16[24,64,1024]{2,1,0:T(8,128)(2,1)} %slice.61, s32[1024]{0:T(1024)S(1)} %pad_clamp_fusion.2), kind=kCustom, calls=%fused_computation.4 | custom fusion | bytes 16777472 | tf_op jit(solution)/shard_map/jit(_take)/gather | solution.py:103
  116.9 1.7 convolution_bitcast_fusion.1
  118.6 7.1 %fusion.4 = f32[1,64,32,64]{3,2,1,0:T(8,128)S(1)} fusion(bf16[64,64,1024]{2,1,0:T(8,128)(2,1)} %gather_fusion.4, bf16[64,32,1152]{2,1,0:T(8,128)(2,1)} %all-to-all-done), kind=kOutput, calls=%fused_computation.21 | convolution fusion | flops 268435456 | bytes 13107200 | tf_op jit(solution)/shard_map/snd,srd->snr/dot_general | solution.py:105
  125.7 1.6 pad_maximum_fusion.2
  127.3 53.8 %all-reduce.2 = bf16[2,64,32,64]{3,2,1,0:T(8,128)(2,1)S(1)} all-reduce(f32[2,64,32,64]{3,2,1,0:T(8,128)} %pad_maximum_fusion.2), channel_id=1, replica_groups=mesh['dz'=8,'dx'=4,'mp'=8] {'mp'}, use_global_device_ids=true, to_apply=%region_20.21 | all-reduce | flops 262144 | bytes 1572864 | tf_op jit(solution)/shard_map/psum | solution.py:107
  181.2 1.6 gather_fusion.7
  182.8 2.1 copy.67
  185.9 4.3 %fusion.10 = bf16[24,64,1152]{2,1,0:T(8,128)(2,1)S(1)} fusion(bf16[24,128,1152]{2,1,0:T(8,128)(2,1)} %bitcast.76, bf16[24,128,64]{1,2,0:T(8,128)(2,1)} %copy.67, pred[24,128]{1,0:T(8,128)(4,1)S(1)} %broadcast_in_dim.118), kind=kOutput, calls=%fused_computation.31 | convolution fusion | flops 453181440 | bytes 11013120 | tf_op jit(solution)/shard_map/pnr,pnd->prd/dot_general | solution.py:128
  190.3 6.2 %select_convert_fusion = bf16[24,64,1152]{2,1,0:T(8,128)(2,1)} fusion(bf16[24,64,1152]{2,1,0:T(8,128)(2,1)S(1)} %fusion.10, bf16[24,128,1152]{2,1,0:T(8,128)(2,1)} %bitcast.77, pred[1152]{0:T(1024)(128)(4,1)S(1)} %iota_compare_fusion.3, bf16[24,128,64]{1,2,0:T(8,128)(2,1)S(1)} %copy.68, pred[24,128]{1,0:T(8,128)(4,1)S(1)} %broadcast_in_dim.118), kind=kOutput, calls=%fused_computation.10 | convolution fusion | flops 454950912 | bytes 14553216 | tf_op jit(solution)/shard_map/pnr,pnd->prd/dot_general | solution.py:131
  196.9 4.6 %convolution_convert_fusion = bf16[64,32,1024]{2,1,0:T(8,128)(2,1)S(1)} fusion(bf16[64,64,1024]{2,1,0:T(8,128)(2,1)} %gather_fusion.4, bf16[2,64,32,64]{3,2,1,0:T(8,128)(2,1)S(1)} %all-reduce.2), kind=kOutput, calls=%fused_computation.16 | convolution fusion | flops 270532608 | bytes 13107200 | tf_op jit(solution)/shard_map/snr,srd->snd/dot_general | solution.py:112
  201.5 2.8 pad_maximum_fusion.1
  204.3 4.9 %all-to-all-start.1 = ((bf16[64,32,1152]{2,1,0:T(8,128)(2,1)}), bf16[64,32,1152]{2,1,0:T(8,128)(2,1)}, u32[]{:S(2)}, u32[]{:S(2)}) async-start(bf16[64,32,1152]{2,1,0:T(8,128)(2,1)} %pad_maximum_fusion.1), calls=%async_computation.2 | async-start | bytes 9437184 | tf_op jit(solution)/shard_map/all_to_all | solution.py:116
  209.3 6.7 %convolution_bitcast_fusion = f32[1024,1024]{1,0:T(8,128)} fusion(bf16[8,1024,128]{2,1,0:T(8,128)(2,1)} %bitcast.102, bf16[1024,1024]{1,0:T(8,128)(2,1)} %param.9), kind=kOutput, calls=%fused_computation.17 | convolution fusion | flops 2147483648 | bytes 8388608 | tf_op jit(solution)/shard_map/krc,dkc->rd/dot_general | solution.py:146
  216.0 47.0 %all-to-all-done.1 = bf16[64,32,1152]{2,1,0:T(8,128)(2,1)} async-done(((bf16[64,32,1152]{2,1,0:T(8,128)(2,1)}), bf16[64,32,1152]{2,1,0:T(8,128)(2,1)}, u32[]{:S(2)}, u32[]{:S(2)}) %all-to-all-start.1) | async-done | bytes 4718624 | tf_op jit(solution)/shard_map/all_to_all | solution.py:116
  263.0 4.6 %gather_fusion.6 = bf16[32,32,1152]{2,1,0:T(8,128)(2,1)} fusion(bf16[64,32,1152]{2,1,0:T(8,128)(2,1)} %all-to-all-done.1, s32[1024]{0:T(1024)S(1)} %pad_clamp_fusion.1), kind=kCustom, calls=%fused_computation.6 | custom fusion | bytes 4718720 | tf_op jit(solution)/shard_map/jit(_take)/gather | solution.py:153
  267.6 1.0 slice.66
  268.8 1.1 fusion.8
  269.9 0.8 copy.69
  270.7 5.0 %add_convert_fusion = bf16[1024,1024]{1,0:T(8,128)(2,1)} fusion(f32[1024,1024]{1,0:T(8,128)} %convolution_bitcast_fusion, bf16[1024,1152]{1,0:T(8,128)(2,1)} %bitcast.80), kind=kLoop, calls=%fused_computation.15 | loop fusion | flops 3145728 | bytes 8388608 | tf_op jit(solution)/shard_map/convert_element_type | solution.py:155
  275.7 1.8 slice.68
  277.5 1.4 slice.69
  (80 shorter events, 9.7 us)
Async XLA Ops:
  7.2 6.2 %copy-start = (bf16[1024,1024]{1,0:T(8,128)(2,1)S(1)}, bf16[1024,1024]{1,0:T(8,128)(2,1)}, u32[]{:S(2)}) copy-start(bf16[1024,1024]{1,0:T(8,128)(2,1)} %param.8) | copy-start | bytes 6291460
  7.2 96.3 %all-gather.5.cloned.1.call-start = ((), (), s32[]{:S(2)}) async-start(), calls=%async_computation.5 | async-start | bytes 3981312 | tf_op jit(solution)/shard_map/all_gather | solution.py:84
  9.2 200.1 %all-gather.7.cloned.1.call-start = ((), (), s32[]{:S(2)}) async-start(), calls=%async_computation.7 | async-start | bytes 2359296 | tf_op jit(solution)/shard_map/all_gather | solution.py:108
  10.0 258.8 %reduce-scatter.3.cloned.1.call-start = ((), (), s32[]{:S(2)}) async-start(), calls=%async_computation.4 | async-start | bytes 4718592 | tf_op jit(solution)/shard_map/reduce_scatter | solution.py:53
  19.4 0.9 copy-start.2
  28.8 5.2 %copy-start.3 = (u32[256]{0:T(256)S(1)}, u32[256]{0:T(256)}, u32[]{:S(2)}) copy-start(u32[256]{0:T(256)} %constant.110) | copy-start | bytes 3076
  28.8 65.9 %all-to-all-start = ((bf16[64,32,1152]{2,1,0:T(8,128)(2,1)}), bf16[64,32,1152]{2,1,0:T(8,128)(2,1)}, u32[]{:S(2)}, u32[]{:S(2)}) async-start(bf16[64,32,1152]{2,1,0:T(8,128)(2,1)} %pad_maximum_fusion), calls=%async_computation.1 | async-start | bytes 9437184 | tf_op jit(solution)/shard_map/all_to_all | solution.py:99
  33.9 241.8 %reduce-scatter.5.cloned.1.call-start = ((), (), s32[]{:S(2)}) async-start(), calls=%async_computation.6 | async-start | bytes 3981312 | tf_op jit(solution)/shard_map/reduce_scatter | solution.py:136
  204.3 58.7 %all-to-all-start.1 = ((bf16[64,32,1152]{2,1,0:T(8,128)(2,1)}), bf16[64,32,1152]{2,1,0:T(8,128)(2,1)}, u32[]{:S(2)}, u32[]{:S(2)}) async-start(bf16[64,32,1152]{2,1,0:T(8,128)(2,1)} %pad_maximum_fusion.1), calls=%async_computation.2 | async-start | bytes 9437184 | tf_op jit(solution)/shard_map/all_to_all | solution.py:116
  269.9 9.0 %copy-start.1 = (bf16[1024,1024]{1,0:T(8,128)(2,1)S(1)}, bf16[1024,1024]{1,0:T(8,128)(2,1)}, u32[]{:S(2)}) copy-start(bf16[1024,1024]{1,0:T(8,128)(2,1)} %param.8) | copy-start | bytes 6291460
Sparse Core Ops, SparseCore 0:
  10.4 47.1 all-gather.4
  59.4 28.2 all-gather.6
  90.3 40.7 reduce-scatter.2
  196.6 44.5 reduce-scatter.4
where the time goes:
time: 286 us; the launch traced here: 285 us
  blocking collectives  110 us (38%)
  waiting for transfers between devices  47.8 us (17%)
  local copies, waits for them, and re-layouts  46.8 us (16%)
  matrix products  37 us (13%)
  other arithmetic  19.2 us (7%)
  between operations  14.7 us (5%)
  starting transfers between devices  10.2 us (4%)
    unnamed x1, blocking collectives  55.9 us
    psum x1, blocking collectives, shards(): both = lax.psum(jnp.stack([down_part, up_part]), 'mp').astype(jnp.bfloat16)  53.8 us
    all_to_all x1, waiting for transfers between devices, shards(): lax.all_to_all(back_send, 'dx', split_axis=0, concat_axis=0, tiled=True)  47 us
    gather x1, local copies, waits for them, and re-layouts, shards(): jnp.take(recv, panel_slot.reshape(-1), axis=0, mode='clip')  8.82 us
    gather x1, local copies, waits for them, and re-layouts, shards(): down_sel = jnp.take(down_col, panel_at, axis=0, mode='clip')  7.48 us
    dot_general x1, matrix products, shards(): jnp.einsum('snd,srd->snr', tok_recv, down_sel, preferred_element_type=jnp...  7.12 us
    dot_general x1, matrix products, shards(): jnp.einsum('krc,dkc->rd', cot_parts, value_weight.reshape(width_loc, n_mp...  6.7 us
    dot_general x1, matrix products, shards(): jnp.einsum('pnr,pnd->prd', by_panel(down_low), rows_p, preferred_element_...  6.16 us
  transfers between devices with their start and end apart: 6, of which 1 were waited for; matrix products, arithmetic and copies ran while one was open for 34% of the time, Pallas kernels for 0%

commit v1 on v0

--- a/solution.py
+++ b/solution.py
@@ -104,7 +104,9 @@
     up_sel = jnp.take(up_col, panel_at, axis=0, mode="clip")
     down_part = jnp.einsum("snd,srd->snr", tok_recv, down_sel, preferred_element_type=jnp.float32)
     up_part = jnp.einsum("snc,src->snr", cot_recv, up_sel, preferred_element_type=jnp.float32)
-    both = lax.psum(jnp.stack([down_part, up_part]), "mp").astype(jnp.bfloat16)
+    both = jnp.sum(lax.all_gather(jnp.stack([down_part, up_part]), axis_name="mp"), 0).astype(
+        jnp.bfloat16
+    )
     cot_parts = lax.all_gather(cotangent, "mp", axis=0, tiled=False)
     down_low = both[0]
     up_grad = both[1]

time: 286 us -> 335 us (1.17); the launches traced: 285 us -> 329 us
  waiting for transfers between devices: 47.8 us -> 142 us
  blocking collectives: 110 us -> 50 us
  other arithmetic: 19.2 us -> 27.7 us
    all_gather x0 -> x1, waiting for transfers between devices: none -> 74.8 us  [shards(): lax.all_gather(jnp.stack([down_part, up_part]), axis_name='mp')]
    psum x1 -> x0, blocking collectives: 53.8 us -> none  [shards(): both = lax.psum(jnp.stack([down_part, up_part]), 'mp').astype(jnp.bfloat16)]
    reduce_scatter x1, waiting for transfers between devices: 0.01 us -> 17.6 us  [shards(): lax.psum_scatter(grads_col.astype(jnp.bfloat16).reshape(column * rank, wi...]
    reduce_sum x0 -> x1, other arithmetic: none -> 8.37 us  [shards(): jnp.sum(lax.all_gather(jnp.stack([down_part, up_part]), axis_name='mp'), 0)]
    unnamed x1, blocking collectives: 55.9 us -> 50 us
  transfers between devices with their start and end apart: 6 -> 7, of which waited for: 1 -> 3; matrix products, arithmetic and copies ran while one was open for 34% -> 29% of each run, Pallas kernels for 0% -> 0%
where the time goes in v1:
time: 335 us; the launch traced here: 329 us
  waiting for transfers between devices  142 us (42%)
  blocking collectives  50 us (15%)
  local copies, waits for them, and re-layouts  46.9 us (14%)
  matrix products  37.2 us (11%)
  other arithmetic  27.7 us (8%)
  between operations  14.7 us (4%)
  starting transfers between devices  10.5 us (3%)
    all_gather x1, waiting for transfers between devices, shards(): lax.all_gather(jnp.stack([down_part, up_part]), axis_name='mp')  74.8 us
    unnamed x1, blocking collectives  50 us
    all_to_all x1, waiting for transfers between devices, shards(): lax.all_to_all(back_send, 'dx', split_axis=0, concat_axis=0, tiled=True)  48.2 us
    reduce_scatter x1, waiting for transfers between devices, shards(): lax.psum_scatter(grads_col.astype(jnp.bfloat16).reshape(column * rank, wi...  17.6 us
    gather x1, local copies, waits for them, and re-layouts, shards(): jnp.take(recv, panel_slot.reshape(-1), axis=0, mode='clip')  8.92 us
    reduce_sum x1, other arithmetic, shards(): jnp.sum(lax.all_gather(jnp.stack([down_part, up_part]), axis_name='mp'), 0)  8.37 us
    gather x1, local copies, waits for them, and re-layouts, shards(): down_sel = jnp.take(down_col, panel_at, axis=0, mode='clip')  7.28 us
    dot_general x1, matrix products, shards(): jnp.einsum('snd,srd->snr', tok_recv, down_sel, preferred_element_type=jnp...  6.97 us
  transfers between devices with their start and end apart: 7, of which 3 were waited for; matrix products, arithmetic and copies ran while one was open for 29% of the time, Pallas kernels for 0%

profile of v1, /device:TPU:224, one launch (start us, length us, event | category | flops | bytes accessed | tf_op | source)
XLA Modules:
  0.0 328.9 jit_solution(1847602955891012609)
XLA Ops:
  7.2 2.0 pad_maximum_fusion.3
  9.9 1.4 gather_fusion
  11.2 1.4 gather_fusion.1
  12.9 1.6 gather_fusion.3
  14.5 2.7 gather_fusion.2
  17.3 5.0 %pad_maximum_fusion = bf16[64,32,1152]{2,1,0:T(8,128)(2,1)} fusion(bf16[64,32,128]{2,1,0:T(8,128)(2,1)S(1)} %gather_fusion.3, bf16[64,32,1024]{2,1,0:T(8,128)(2,1)} %gather_fusion.2), kind=kLoop, calls=%fused_computation.11 | loop fusion | flops 9437184 | bytes 9437184 | tf_op jit(solution)/shard_map/concatenate | solution.py:92
  22.2 5.0 %all-to-all-start = ((bf16[64,32,1152]{2,1,0:T(8,128)(2,1)}), bf16[64,32,1152]{2,1,0:T(8,128)(2,1)}, u32[]{:S(2)}, u32[]{:S(2)}) async-start(bf16[64,32,1152]{2,1,0:T(8,128)(2,1)} %pad_maximum_fusion), calls=%async_computation.1 | async-start | bytes 9437184 | tf_op jit(solution)/shard_map/all_to_all | solution.py:99
  27.3 5.9 %fusion.27 = f32[1024,1024]{1,0:T(8,128)} fusion(bf16[1024,1024]{1,0:T(8,128)(2,1)} %param.9, bf16[1024,1024]{1,0:T(8,128)(2,1)S(1)} %copy-done), kind=kOutput, calls=%fused_computation.109 | convolution fusion | flops 2147483648 | bytes 8388608 | tf_op jit(solution)/shard_map/dot_general | solution.py:49
  34.7 50.0 %all-reduce = s32[128]{0:T(128)S(1)} all-reduce(s32[128]{0:T(128)S(1)} %dynamic-update-slice), channel_id=2, replica_groups=mesh['dz'=8,'dx'=4,'mp'=8] {'dx'}, use_global_device_ids=true, to_apply=%add | all-reduce | flops 128 | bytes 1024
  89.1 4.0 %slice.61 = bf16[24,64,1024]{2,1,0:T(8,128)(2,1)} slice(bf16[24,64,1152]{2,1,0:T(8,128)(2,1)} %all-gather.7.cloned.1.call-done), slice={[0:24], [0:64], [0:1024]} | slice | bytes 6291456 | tf_op jit(solution)/shard_map/slice | solution.py:87
  93.2 7.3 %gather_fusion.4 = bf16[64,64,1024]{2,1,0:T(8,128)(2,1)} fusion(bf16[24,64,1024]{2,1,0:T(8,128)(2,1)} %slice.61, s32[1024]{0:T(1024)S(1)} %pad_clamp_fusion.2), kind=kCustom, calls=%fused_computation.4 | custom fusion | bytes 16777472 | tf_op jit(solution)/shard_map/jit(_take)/gather | solution.py:103
  100.5 1.7 convolution_bitcast_fusion.1
  102.1 7.0 %fusion.4 = f32[1,64,32,64]{3,2,1,0:T(8,128)S(1)} fusion(bf16[64,64,1024]{2,1,0:T(8,128)(2,1)} %gather_fusion.4, bf16[64,32,1152]{2,1,0:T(8,128)(2,1)} %all-to-all-done), kind=kOutput, calls=%fused_computation.21 | convolution fusion | flops 268435456 | bytes 13107200 | tf_op jit(solution)/shard_map/snd,srd->snr/dot_general | solution.py:105
  109.1 1.6 pad_maximum_fusion.2
  112.9 8.9 %gather_fusion.8 = bf16[96,32,1152]{2,1,0:T(8,128)(2,1)} fusion(bf16[64,32,1152]{2,1,0:T(8,128)(2,1)} %all-to-all-done, s32[1024]{0:T(1024)S(1)} %pad_clamp_fusion), kind=kCustom, calls=%fused_computation.8 | custom fusion | bytes 14156160 | tf_op jit(solution)/shard_map/jit(_take)/gather | solution.py:127
  121.9 74.8 %all-gather.9.cloned.1.call-done = f32[16,64,32,64]{3,2,1,0:T(8,128)} async-done(((f32[2,64,32,64]{3,2,1,0:T(8,128)}), f32[16,64,32,64]{3,2,1,0:T(8,128)}) %all-gather.9.cloned.1.call-update) | async-done | bytes 8388624 | tf_op jit(solution)/shard_map/all_gather | solution.py:107
  196.7 8.4 %reduce_sum.210 = bf16[2,64,32,64]{3,2,1,0:T(8,128)(2,1)S(1)} reduce(f32[8,2,64,32,64]{4,3,2,1,0:T(8,128)} %bitcast.79, f32[]{:T(128)} %constant.105.clone.1), dimensions={0}, to_apply=%region_20.21 | reduce | flops 1835008 | bytes 8912900 | tf_op jit(solution)/shard_map/reduce_sum | solution.py:107
  205.1 1.6 gather_fusion.7
  206.7 2.1 copy.67
  209.9 4.6 %fusion.10 = bf16[24,64,1152]{2,1,0:T(8,128)(2,1)S(1)} fusion(bf16[24,128,1152]{2,1,0:T(8,128)(2,1)} %bitcast.77, bf16[24,128,64]{1,2,0:T(8,128)(2,1)} %copy.67, pred[24,128]{1,0:T(8,128)(4,1)S(1)} %broadcast_in_dim.118), kind=kOutput, calls=%fused_computation.31 | convolution fusion | flops 453181440 | bytes 11013120 | tf_op jit(solution)/shard_map/pnr,pnd->prd/dot_general | solution.py:130
  214.5 6.2 %select_convert_fusion = bf16[24,64,1152]{2,1,0:T(8,128)(2,1)} fusion(bf16[24,64,1152]{2,1,0:T(8,128)(2,1)S(1)} %fusion.10, bf16[24,128,1152]{2,1,0:T(8,128)(2,1)} %bitcast.78, pred[1152]{0:T(1024)(128)(4,1)S(1)} %iota_compare_fusion.3, bf16[24,128,64]{1,2,0:T(8,128)(2,1)S(1)} %copy.68, pred[24,128]{1,0:T(8,128)(4,1)S(1)} %broadcast_in_dim.118), kind=kOutput, calls=%fused_computation.10 | convolution fusion | flops 454950912 | bytes 14553216 | tf_op jit(solution)/shard_map/pnr,pnd->prd/dot_general | solution.py:133
  221.1 4.7 %convolution_convert_fusion = bf16[64,32,1024]{2,1,0:T(8,128)(2,1)S(1)} fusion(bf16[64,64,1024]{2,1,0:T(8,128)(2,1)} %gather_fusion.4, bf16[2,64,32,64]{3,2,1,0:T(8,128)(2,1)S(1)} %reduce_sum.210), kind=kOutput, calls=%fused_computation.16 | convolution fusion | flops 270532608 | bytes 13107200 | tf_op jit(solution)/shard_map/snr,srd->snd/dot_general | solution.py:114
  225.9 2.8 pad_maximum_fusion.1
  228.7 5.2 %all-to-all-start.1 = ((bf16[64,32,1152]{2,1,0:T(8,128)(2,1)}), bf16[64,32,1152]{2,1,0:T(8,128)(2,1)}, u32[]{:S(2)}, u32[]{:S(2)}) async-start(bf16[64,32,1152]{2,1,0:T(8,128)(2,1)} %pad_maximum_fusion.1), calls=%async_computation.2 | async-start | bytes 9437184 | tf_op jit(solution)/shard_map/all_to_all | solution.py:118
  233.9 6.7 %convolution_bitcast_fusion = f32[1024,1024]{1,0:T(8,128)} fusion(bf16[8,1024,128]{2,1,0:T(8,128)(2,1)} %bitcast.104, bf16[1024,1024]{1,0:T(8,128)(2,1)} %param.9), kind=kOutput, calls=%fused_computation.17 | convolution fusion | flops 2147483648 | bytes 8388608 | tf_op jit(solution)/shard_map/krc,dkc->rd/dot_general | solution.py:148
  240.5 48.2 %all-to-all-done.1 = bf16[64,32,1152]{2,1,0:T(8,128)(2,1)} async-done(((bf16[64,32,1152]{2,1,0:T(8,128)(2,1)}), bf16[64,32,1152]{2,1,0:T(8,128)(2,1)}, u32[]{:S(2)}, u32[]{:S(2)}) %all-to-all-start.1) | async-done | bytes 4718624 | tf_op jit(solution)/shard_map/all_to_all | solution.py:118
  288.8 4.6 %gather_fusion.6 = bf16[32,32,1152]{2,1,0:T(8,128)(2,1)} fusion(bf16[64,32,1152]{2,1,0:T(8,128)(2,1)} %all-to-all-done.1, s32[1024]{0:T(1024)S(1)} %pad_clamp_fusion.1), kind=kCustom, calls=%fused_computation.6 | custom fusion | bytes 4718720 | tf_op jit(solution)/shard_map/jit(_take)/gather | solution.py:155
  294.5 1.1 fusion.8
  296.5 5.0 %add_convert_fusion = bf16[1024,1024]{1,0:T(8,128)(2,1)} fusion(f32[1024,1024]{1,0:T(8,128)} %convolution_bitcast_fusion, bf16[1024,1152]{1,0:T(8,128)(2,1)} %bitcast.82), kind=kLoop, calls=%fused_computation.15 | loop fusion | flops 3145728 | bytes 8388608 | tf_op jit(solution)/shard_map/convert_element_type | solution.py:157
  301.5 17.6 %reduce-scatter.5.cloned.1.call-done = bf16[192,1152]{1,0:T(8,128)(2,1)} async-done(((bf16[1536,1152]{1,0:T(8,128)(2,1)}), bf16[192,1152]{1,0:T(8,128)(2,1)}) %reduce-scatter.5.cloned.1.call-update) | async-done | bytes 442384 | tf_op jit(solution)/shard_map/reduce_scatter | solution.py:138
  319.2 1.8 slice.68
  320.9 1.4 slice.69
  (81 shorter events, 12.0 us)
Async XLA Ops:
  7.2 7.4 %copy-start = (bf16[1024,1024]{1,0:T(8,128)(2,1)S(1)}, bf16[1024,1024]{1,0:T(8,128)(2,1)}, u32[]{:S(2)}) copy-start(bf16[1024,1024]{1,0:T(8,128)(2,1)} %param.8) | copy-start | bytes 6291460
  7.2 80.2 %all-gather.7.cloned.1.call-start = ((), (), s32[]{:S(2)}) async-start(), calls=%async_computation.5 | async-start | bytes 3981312 | tf_op jit(solution)/shard_map/all_gather | solution.py:84
  22.2 78.2 %all-to-all-start = ((bf16[64,32,1152]{2,1,0:T(8,128)(2,1)}), bf16[64,32,1152]{2,1,0:T(8,128)(2,1)}, u32[]{:S(2)}, u32[]{:S(2)}) async-start(bf16[64,32,1152]{2,1,0:T(8,128)(2,1)} %pad_maximum_fusion), calls=%async_computation.1 | async-start | bytes 9437184 | tf_op jit(solution)/shard_map/all_to_all | solution.py:99
  27.2 169.5 %all-gather.9.cloned.1.call-start = ((), (), s32[]{:S(2)}) async-start(), calls=%async_computation.7 | async-start | bytes 18874368 | tf_op jit(solution)/shard_map/all_gather | solution.py:107
  27.3 6.0 %copy-start.2 = (u32[256]{0:T(256)S(1)}, u32[256]{0:T(256)}, u32[]{:S(2)}) copy-start(u32[256]{0:T(256)} %constant.112) | copy-start | bytes 3076
  110.7 123.2 %all-gather.11.cloned.1.call-start = ((), (), s32[]{:S(2)}) async-start(), calls=%async_computation.8 | async-start | bytes 2359296 | tf_op jit(solution)/shard_map/all_gather | solution.py:110
  111.5 183.1 %reduce-scatter.3.cloned.1.call-start = ((), (), s32[]{:S(2)}) async-start(), calls=%async_computation.4 | async-start | bytes 4718592 | tf_op jit(solution)/shard_map/reduce_scatter | solution.py:53
  112.0 207.1 %reduce-scatter.5.cloned.1.call-start = ((), (), s32[]{:S(2)}) async-start(), calls=%async_computation.6 | async-start | bytes 3981312 | tf_op jit(solution)/shard_map/reduce_scatter | solution.py:138
  228.7 60.1 %all-to-all-start.1 = ((bf16[64,32,1152]{2,1,0:T(8,128)(2,1)}), bf16[64,32,1152]{2,1,0:T(8,128)(2,1)}, u32[]{:S(2)}, u32[]{:S(2)}) async-start(bf16[64,32,1152]{2,1,0:T(8,128)(2,1)} %pad_maximum_fusion.1), calls=%async_computation.2 | async-start | bytes 9437184 | tf_op jit(solution)/shard_map/all_to_all | solution.py:118
  295.6 26.7 %copy-start.1 = (bf16[1024,1024]{1,0:T(8,128)(2,1)S(1)}, bf16[1024,1024]{1,0:T(8,128)(2,1)}, u32[]{:S(2)}) copy-start(bf16[1024,1024]{1,0:T(8,128)(2,1)} %param.8) | copy-start | bytes 6291460
Sparse Core Ops, SparseCore 0:
  10.4 47.1 all-gather.6
  110.8 85.7 all-gather.8
  198.5 28.3 all-gather.10
  229.3 41.5 reduce-scatter.2
  273.3 45.7 reduce-scatter.4
